TPU v7x, 32 devices: a whole 2x2x4 slice. The times are simulated.
32 devices in a mesh: row: 2 (over y), col: 16 (over z, x, core).
Axes of the slice: x: 2, y: 2, z: 4, core: 2. Of those that a mesh axis runs over, the one named last changes fastest.
Arguments:
- object_field: float32 [2, 512, 4096], P(None, 'row', 'col'), may hold values from -5 to 5
- probe: float32 [2, 2, 256, 256], replicated, may hold values from -5 to 5
- amplitudes: float32 [2, 16, 1, 256, 256], P('row', 'col'), may hold values from 0.5 to 3
- offsets: int32 [2, 16, 1, 2], P('row', 'col'), may hold values from 0 to 128
Outputs:
- new_object: float32 [2, 512, 4096], P(None, 'row', 'col')
- new_probe: float32 [2, 2, 256, 256], replicated
All inputs are finite; a program needn't handle non-finite values.
Results may differ from a plain program's by a relative error of at most 0.0003.
Values sent between devices are 32-bit elements; how exact they have to be, the bound alone decides.
A program may use at most 64 MiB of HBM per device.

v0:
```python
import functools
import math

import jax
import jax.numpy as jnp
import numpy as np
from jax import lax
from jax.experimental import pallas as pl
from jax.experimental.pallas import tpu as pltpu
from jax.sharding import PartitionSpec as P

H = 64
LANES = 128
ITERS = 2
object_step = 0.25
probe_step = 4.0
MESH = pl.DeviceIdType.MESH
bf16 = jnp.bfloat16


def dft_tables(length):
    counter = np.arange(length)
    angle = -2.0 * math.pi / length * (counter[:, None] * counter[None, :] % length)
    scale = 1.0 / math.sqrt(length)
    parts = []
    for table in (np.cos(angle) * scale, np.sin(angle) * scale):
        table = table.astype(np.float32)
        high = table.astype(bf16)
        low = (table - high.astype(np.float32)).astype(bf16)
        parts += [high, low]
    return np.stack(parts)


def split(value):
    high = value.astype(bf16)
    return high, (value - high.astype(jnp.float32)).astype(bf16)


def product(left, right):
    out = jnp.dot(left[0][...], right[0][...], preferred_element_type=jnp.float32)
    out += jnp.dot(left[0][...], right[1][...], preferred_element_type=jnp.float32)
    return out + jnp.dot(left[1][...], right[0][...], preferred_element_type=jnp.float32)


def pick(one_hot, value):
    if isinstance(value, tuple):
        return sum(jnp.dot(one_hot[...], v, preferred_element_type=jnp.float32) for v in value)
    return sum(jnp.dot(v, value[...], preferred_element_type=jnp.float32) for v in one_hot)


def kernel(
    rows, cols, obj_ref, probe_ref, amp_ref, tables_ref, off_ref,
    new_obj_ref, new_probe_ref,
    a_hi, a_lo, b_hi, b_lo, x_hi, x_lo,
    row_pick, col_pick, row_place, col_place, ext, side, pack, grad, gpack, grows, gside, gcorner, current,
    terms, r1, a1, r2, a2, r3, weights,
    halo_send, halo_recv, grad_send, grad_recv, sum_send, sum_recv,
):
    frame = amp_ref.shape[-1]
    tile = obj_ref.shape[1]
    modes = probe_ref.shape[1]
    span = tile + 2 * H
    row, col = lax.axis_index("row"), lax.axis_index("col")
    coeff = probe_step / (rows * cols)
    core = lax.rem(col, 2)
    plane = row * 2 + lax.rem(col // 2, 2)
    line = col // 4
    planes, lines = rows * 2, cols // 4

    around = [(dr, dc) for dr in (-1, 0, 1) for dc in (-1, 0, 1) if (dr, dc) != (0, 0)]

    def inside(dr, dc):
        r, c = row + dr, col + dc
        ok = jnp.bool_(True)
        if dr:
            ok = (r >= 0) & (r < rows)
        if dc:
            ok = ok & (c >= 0) & (c < cols)
        return ok

    def plane_peer(d):
        other = lax.rem(plane + d, planes)
        return (other // 2, line * 4 + lax.rem(other, 2) * 2 + core), other

    def line_peer(d):
        other = lax.rem(line + d, lines)
        return (row, other * 4 + lax.rem(col, 4)), other

    partner = (row, col + 1 - 2 * core)

    ext[...] = jnp.zeros_like(ext)
    side[...] = jnp.zeros_like(side)
    grows[...] = jnp.zeros_like(grows)
    gside[...] = jnp.zeros_like(gside)
    gcorner[...] = jnp.zeros_like(gcorner)

    barrier = pltpu.get_barrier_semaphore()
    for dr, dc in around:
        @pl.when(inside(dr, dc))
        def _(dr=dr, dc=dc):
            pl.semaphore_signal(barrier, inc=1, device_id=(row + dr, col + dc), device_id_type=MESH)
    pl.semaphore_signal(barrier, inc=1, device_id=partner, device_id_type=MESH)
    for d in range(1, planes):
        pl.semaphore_signal(barrier, inc=1, device_id=plane_peer(d)[0], device_id_type=MESH)
    for d in range(1, lines):
        pl.semaphore_signal(barrier, inc=1, device_id=line_peer(d)[0], device_id_type=MESH)

    lane = lax.broadcasted_iota(jnp.int32, (1, LANES), 1)
    lower, upper = lane < H, lane >= H

    def paired(mask, real, imag):
        return jnp.where(mask, real, pltpu.roll(imag, H, 1))

    def pack_tile(k, src):
        pack[k, 0] = paired(lower, src[0, :, :LANES], src[1, :, :LANES])
        pack[k, 1] = paired(upper, src[0, :, tile - LANES:], src[1, :, tile - LANES:])

    def halo_copy(k, src, dr, dc):
        n = around.index((dr, dc))
        if dc == 0:
            source = src.at[:, pl.ds(0 if dr < 0 else tile - H, H), :]
            target = ext.at[k, :, pl.ds(tile + H if dr < 0 else 0, H), pl.ds(LANES, tile)]
        else:
            which = 0 if dc < 0 else 1
            at, size = {-1: (0, H), 0: (0, tile), 1: (tile - H, H)}[dr]
            source = pack.at[k, which, pl.ds(at, size)]
            target = side.at[k, 1 - which, pl.ds({-1: tile + H, 0: H, 1: 0}[dr], size)]
        return pltpu.make_async_remote_copy(
            src_ref=source, dst_ref=target, send_sem=halo_send.at[k, n], recv_sem=halo_recv.at[k, n],
            device_id=(row + dr, col + dc), device_id_type=MESH)

    def grad_copy(k, dr, dc):
        n = around.index((dr, dc))
        if dc == 0:
            source = grad.at[k, :, pl.ds(0 if dr < 0 else tile + H, H), pl.ds(LANES, tile)]
            target = grows.at[k, 0 if dr > 0 else 1]
        else:
            which = 0 if dc < 0 else 1
            at, size = {-1: (0, H), 0: (H, tile), 1: (tile + H, H)}[dr]
            source = gpack.at[k, which, pl.ds(at, size)]
            if dr == 0:
                target = gside.at[k, 1 - which]
            else:
                target = gcorner.at[k, 1 - which, 0 if dr > 0 else 1]
        return pltpu.make_async_remote_copy(
            src_ref=source, dst_ref=target, send_sem=grad_send.at[k, n], recv_sem=grad_recv.at[k, n],
            device_id=(row + dr, col + dc), device_id_type=MESH)

    def start_all(make):
        for dr, dc in around:
            @pl.when(inside(dr, dc))
            def _(dr=dr, dc=dc):
                make(dr, dc).start()

    def wait_all(make, send):
        for dr, dc in around:
            if send:
                @pl.when(inside(dr, dc))
                def _(dr=dr, dc=dc):
                    make(dr, dc).wait_send()
            else:
                @pl.when(inside(-dr, -dc))
                def _(dr=dr, dc=dc):
                    make(dr, dc).wait_recv()

    pack_tile(0, obj_ref)
    tall = 1 + (row > 0).astype(jnp.int32) + (row < rows - 1).astype(jnp.int32)
    broad = 1 + (col > 0).astype(jnp.int32) + (col < cols - 1).astype(jnp.int32)
    pl.semaphore_wait(barrier, tall * broad - 1 + planes + lines - 1)
    start_all(lambda dr, dc: halo_copy(0, obj_ref, dr, dc))

    for n, (a, b) in enumerate(((a_hi, b_hi), (a_lo, b_lo))):
        real, imag = tables_ref[n], tables_ref[2 + n]
        lo, hi = pl.ds(0, frame), pl.ds(frame, frame)
        for ref, sign in ((a, 1), (b, -1)):
            ref[lo, lo] = real
            ref[hi, hi] = real
            ref[lo, hi] = -imag if sign > 0 else imag
            ref[hi, lo] = imag if sign > 0 else -imag
    half = frame // LANES
    for c in range(2):
        ext[0, c, H:H + tile, LANES:LANES + tile] = obj_ref[c]
        for m in range(modes):
            for h in range(half):
                weights[0, pl.ds(((c * modes + m) * half + h) * frame, frame)] = (
                    probe_ref[c, m, :, h * LANES:(h + 1) * LANES])

    def probe_part(k, c, m):
        base = (c * modes + m) * half
        return jnp.concatenate(
            [weights[k, pl.ds((base + h) * frame, frame)] for h in range(half)], axis=1)

    oy, ox = off_ref[0, 0, 0, 0], off_ref[0, 0, 0, 1] + (LANES - H)
    for ref, outer, shift in (
        (row_pick, 0, oy), (row_place, 1, oy), (col_pick, 1, ox), (col_place, 0, ox)
    ):
        inner_at = lax.broadcasted_iota(jnp.int32, ref.shape, outer)
        outer_at = lax.broadcasted_iota(jnp.int32, ref.shape, 1 - outer)
        ref[...] = jnp.where(outer_at == inner_at + shift, 1.0, 0.0).astype(bf16)

    for k in range(ITERS):
        source = obj_ref if k == 0 else current
        wait_all(lambda dr, dc: halo_copy(k, source, dr, dc), False)
        for s, at in ((0, 0), (1, LANES + tile)):
            block = side[k, s]
            other = pltpu.roll(block, H, 1)
            first, second = (block, other)
            ext[k, 0, :, at:at + LANES] = first
            ext[k, 1, :, at:at + LANES] = second
        patch = [
            pick(split(pick(row_pick, split(ext[k, c]))), col_pick)
            for c in range(2)
        ]

        def cut(m):
            return pl.ds(m * frame, frame)

        for m in range(modes):
            p_re, p_im = probe_part(k, 0, m), probe_part(k, 1, m)
            for c, wave in enumerate((p_re * patch[0] - p_im * patch[1], p_re * patch[1] + p_im * patch[0])):
                x_hi[cut(c), cut(m)], x_lo[cut(c), cut(m)] = split(wave)
        out = product((a_hi, a_lo), (x_hi, x_lo))
        for m in range(modes):
            for c in range(2):
                part = out[c * frame:(c + 1) * frame, m * frame:(m + 1) * frame]
                x_hi[cut(m), cut(c)], x_lo[cut(m), cut(c)] = split(part)
        far = product((x_hi, x_lo), (b_hi, b_lo))
        far = [[far[m * frame:(m + 1) * frame, c * frame:(c + 1) * frame] for c in range(2)] for m in range(modes)]
        intensity = sum(re * re + im * im for re, im in far)
        factor = 1.0 - amp_ref[0, 0, 0] / jnp.sqrt(intensity + 1.0)
        for m in range(modes):
            for c in range(2):
                x_hi[cut(m), cut(c)], x_lo[cut(m), cut(c)] = split(far[m][c] * factor)
        out = product((x_hi, x_lo), (a_hi, a_lo))
        for m in range(modes):
            for c in range(2):
                part = out[m * frame:(m + 1) * frame, c * frame:(c + 1) * frame]
                x_hi[cut(c), cut(m)], x_lo[cut(c), cut(m)] = split(part)
        back = product((b_hi, b_lo), (x_hi, x_lo))
        back = [[back[c * frame:(c + 1) * frame, m * frame:(m + 1) * frame] for c in range(2)] for m in range(modes)]

        for m in range(modes):
            re, im = back[m]
            for c, term in enumerate((patch[0] * re + patch[1] * im, patch[0] * im - patch[1] * re)):
                for h in range(half):
                    terms[k, pl.ds(((c * modes + m) * half + h) * frame, frame)] = term[:, h * LANES:(h + 1) * LANES]
        total = terms.shape[1]
        n1 = total // 2
        n2 = n1 // planes
        n3 = n2 // lines

        def remote(src, dst, slot, device):
            return pltpu.make_async_remote_copy(
                src_ref=src, dst_ref=dst, send_sem=sum_send.at[k, slot], recv_sem=sum_recv.at[k, slot],
                device_id=device, device_id_type=MESH)

        swap = remote(terms.at[k, pl.ds(pl.multiple_of((1 - core) * n1, 8), n1)], r1.at[k], 0, partner)
        swap.start()

        for c in range(2):
            acc = None
            for m in range(modes):
                p_re, p_im = probe_part(k, 0, m), probe_part(k, 1, m)
                re, im = back[m]
                term = p_re * re + p_im * im if c == 0 else p_re * im - p_im * re
                acc = term if acc is None else acc + term
            grad[k, c] = pick(split(pick(row_place, split(acc))), col_place)
        gpack[k, 0] = paired(upper, grad[k, 0, :, :LANES], grad[k, 1, :, :LANES])
        gpack[k, 1] = paired(lower, grad[k, 0, :, LANES + tile:], grad[k, 1, :, LANES + tile:])
        start_all(lambda dr, dc: grad_copy(k, dr, dc))

        swap.wait_recv()
        a1[k] = terms[k, pl.ds(pl.multiple_of(core * n1, 8), n1)] + r1[k]
        slot = 1
        scatter2 = []
        for d in range(1, planes):
            device, other = plane_peer(d)
            copy = remote(a1.at[k, pl.ds(pl.multiple_of(other * n2, 8), n2)], r2.at[k, d - 1], slot, device)
            copy.start()
            scatter2.append(copy)
            slot += 1

        wait_all(lambda dr, dc: grad_copy(k, dr, dc), False)
        target = current if k + 1 < ITERS else new_obj_ref
        for s in range(2):
            mask, at = ((lower, 0), (upper, tile - LANES))[s]
            block = gside[k, s]
            block = jnp.concatenate(
                [block[:H] + gcorner[k, s, 0], block[H:tile - H], block[tile - H:] + gcorner[k, s, 1]], axis=0)
            where = pl.ds(LANES + at, LANES)
            grad[k, 0, H:H + tile, where] += jnp.where(mask, block, 0.0)
            grad[k, 1, H:H + tile, where] += jnp.where(mask, pltpu.roll(block, H, 1), 0.0)
        grad[k, :, H:2 * H, LANES:LANES + tile] += grows[k, 0]
        grad[k, :, tile:tile + H, LANES:LANES + tile] += grows[k, 1]
        for c in range(2):
            target[c] = source[c] - object_step * grad[k, c, H:H + tile, LANES:LANES + tile]
        if k + 1 < ITERS:
            pack_tile(k + 1, current)
            start_all(lambda dr, dc: halo_copy(k + 1, current, dr, dc))
            for c in range(2):
                ext[k + 1, c, H:H + tile, LANES:LANES + tile] = current[c]

        for copy in scatter2:
            copy.wait_recv()
        value = a1[k, pl.ds(pl.multiple_of(plane * n2, 8), n2)]
        for d in range(1, planes):
            value = value + r2[k, d - 1]
        a2[k] = value
        scatter3 = []
        for d in range(1, lines):
            device, other = line_peer(d)
            copy = remote(a2.at[k, pl.ds(pl.multiple_of(other * n3, 8), n3)], r3.at[k, d - 1], slot, device)
            copy.start()
            scatter3.append(copy)
            slot += 1
        for copy in scatter3:
            copy.wait_recv()
        value = a2[k, pl.ds(pl.multiple_of(line * n3, 8), n3)]
        for d in range(1, lines):
            value = value + r3[k, d - 1]
        at1 = core * n1
        at2 = at1 + plane * n2
        at3 = at2 + line * n3
        mine = pl.ds(pl.multiple_of(at3, 8), n3)
        weights[k + 1, mine] = weights[k, mine] - coeff * value

        gathers = []
        for peers, make, at, size in (
            (lines, line_peer, at3, n3), (planes, plane_peer, at2, n2), (2, lambda d: (partner, None), at1, n1)
        ):
            block = weights.at[k + 1, pl.ds(pl.multiple_of(at, 8), size)]
            stage = []
            for d in range(1, peers):
                copy = remote(block, block, slot, make(d)[0])
                copy.start()
                stage.append(copy)
                slot += 1
            for copy in stage:
                copy.wait_recv()
            gathers += stage
        for copy in [swap] + scatter2 + scatter3 + gathers:
            copy.wait_send()
        wait_all(lambda dr, dc: halo_copy(k, source, dr, dc), True)
        wait_all(lambda dr, dc: grad_copy(k, dr, dc), True)

    for c in range(2):
        for m in range(modes):
            new_probe_ref[c, m] = probe_part(ITERS, c, m)


def local(rows, cols, object_field, probe, amplitudes, offsets):
    frame = amplitudes.shape[-1]
    tile = object_field.shape[1]
    modes = probe.shape[1]
    span, width = tile + 2 * H, tile + 2 * LANES
    tables = jnp.asarray(dft_tables(frame))
    total = 2 * modes * frame * (frame // LANES)
    planes, lines = rows * 2, cols // 4
    n1 = total // 2
    n2 = n1 // planes
    n3 = n2 // lines
    copies = 2 + 2 * (planes - 1) + 2 * (lines - 1)
    f32 = jnp.float32
    wide = 2 * frame
    vmem = pl.BlockSpec(memory_space=pltpu.VMEM)
    dma = pltpu.SemaphoreType.DMA
    return pl.pallas_call(
        functools.partial(kernel, rows, cols),
        out_shape=(
            jax.ShapeDtypeStruct(object_field.shape, f32),
            jax.ShapeDtypeStruct(probe.shape, f32),
        ),
        in_specs=[vmem] * 4 + [pl.BlockSpec(memory_space=pltpu.SMEM)],
        out_specs=(vmem, vmem),
        scratch_shapes=[
            *[pltpu.VMEM((wide, wide), bf16)] * 4,
            *[pltpu.VMEM((wide, modes * frame), bf16)] * 2,
            pltpu.VMEM((frame, span), bf16),
            pltpu.VMEM((width, frame), bf16),
            pltpu.VMEM((span, frame), bf16),
            pltpu.VMEM((frame, width), bf16),
            pltpu.VMEM((ITERS, 2, span, width), f32),
            pltpu.VMEM((ITERS, 2, span, LANES), f32),
            pltpu.VMEM((ITERS, 2, tile, LANES), f32),
            pltpu.VMEM((ITERS, 2, span, width), f32),
            pltpu.VMEM((ITERS, 2, span, LANES), f32),
            pltpu.VMEM((ITERS, 2, 2, H, tile), f32),
            pltpu.VMEM((ITERS, 2, tile, LANES), f32),
            pltpu.VMEM((ITERS, 2, 2, H, LANES), f32),
            pltpu.VMEM((2, tile, tile), f32),
            pltpu.VMEM((ITERS, total, LANES), f32),
            pltpu.VMEM((ITERS, n1, LANES), f32),
            pltpu.VMEM((ITERS, n1, LANES), f32),
            pltpu.VMEM((ITERS, planes - 1, n2, LANES), f32),
            pltpu.VMEM((ITERS, n2, LANES), f32),
            pltpu.VMEM((ITERS, lines - 1, n3, LANES), f32),
            pltpu.VMEM((ITERS + 1, total, LANES), f32),
            dma((ITERS, 8)), dma((ITERS, 8)), dma((ITERS, 8)), dma((ITERS, 8)),
            dma((ITERS, copies)), dma((ITERS, copies)),
        ],
        compiler_params=pltpu.CompilerParams(
            collective_id=0, has_side_effects=True, vmem_limit_bytes=60 * 1024 * 1024
        ),
    )(object_field, probe, amplitudes, tables, offsets)


def solution(mesh):
    rows, cols = mesh.shape["row"], mesh.shape["col"]

    def body(*args):
        return local(rows, cols, *args)

    return jax.shard_map(
        body,
        mesh=mesh,
        in_specs=(
            P(None, "row", "col"),
            P(),
            P("row", "col", None, None, None),
            P("row", "col", None, None),
        ),
        out_specs=(P(None, "row", "col"), P()),
        check_vma=False,
    )
```

profile of v0, /device:TPU:0, one launch (start us, length us, event | category | flops | bytes accessed | tf_op | source)
XLA Modules:
  0.0 90.1 jit_solution(4551298631598485599)
XLA Ops:
  0.6 86.5 %shard_map.68 = (f32[2,256,256]{2,1,0:T(8,128)}, f32[2,2,256,256]{3,2,1,0:T(8,128)}) custom-call(f32[2,256,256]{2,1,0:T(8,128)} %obj_ref.1, f32[2,2,256,256]{3,2,1,0:T(8,128)} %probe_ref.1, f32[1,1,1,256,256]{4,3,2,1,0:T(8,128)} %amp_ref.1, bf16[4,256,256]{2,1,0:T(8,128)(2,1)} %constant.2.clone.tables_ref, s32[1,1,1,2]{3,2,1,0:T(1,128)} %off_ref.1), custom_call_target="tpu_custom_call" | custom-call | tf_op jit(solution)/shard_map/pallas_call | solution.py:367
  87.1 0.0 copy-start
  87.1 2.0 %copy.9 = f32[2,256,256]{2,1,0:T(8,128)} copy(f32[2,256,256]{2,1,0:T(8,128)} %get-tuple-element.4) | data formatting | bytes 1048576
  89.1 0.0 copy-done
  89.1 1.0 %copy.10 = f32[2,2,256,256]{3,2,1,0:T(8,128)} copy(f32[2,2,256,256]{3,2,1,0:T(8,128)S(1)} %copy-done) | data formatting | bytes 2097152
Async XLA Ops:
  87.1 2.0 %copy-start = (f32[2,2,256,256]{3,2,1,0:T(8,128)S(1)}, f32[2,2,256,256]{3,2,1,0:T(8,128)}, u32[]{:S(2)}) copy-start(f32[2,2,256,256]{3,2,1,0:T(8,128)} %get-tuple-element.5) | copy-start | bytes 3145732
where the time goes:
time: 90.2 us; the launch traced here: 90.1 us
  Pallas kernels  86.5 us (96%)
  local copies, waits for them, and re-layouts  2.93 us (3%)
    pallas_call x1, Pallas kernels, local(): pl.pallas_call(functools.partial(kernel, rows, cols), out_shape=(jax.Shap...  86.5 us
    unnamed x4, local copies, waits for them, and re-layouts  2.93 us

commit v1 on v0

--- a/solution.py
+++ b/solution.py
@@ -78,12 +78,20 @@
             ok = ok & (c >= 0) & (c < cols)
         return ok
 
+    def flip(index, d):
+        bit = 1
+        while bit <= d:
+            if d & bit:
+                index = index + bit * (1 - 2 * lax.rem(index // bit, 2))
+            bit *= 2
+        return index
+
     def plane_peer(d):
-        other = lax.rem(plane + d, planes)
+        other = flip(plane, d)
         return (other // 2, line * 4 + lax.rem(other, 2) * 2 + core), other
 
     def line_peer(d):
-        other = lax.rem(line + d, lines)
+        other = flip(line, d)
         return (row, other * 4 + lax.rem(col, 4)), other
 
     partner = (row, col + 1 - 2 * core)
@@ -244,18 +252,31 @@
             for c, term in enumerate((patch[0] * re + patch[1] * im, patch[0] * im - patch[1] * re)):
                 for h in range(half):
                     terms[k, pl.ds(((c * modes + m) * half + h) * frame, frame)] = term[:, h * LANES:(h + 1) * LANES]
-        total = terms.shape[1]
-        n1 = total // 2
-        n2 = n1 // planes
-        n3 = n2 // lines
-
-        def remote(src, dst, slot, device):
-            return pltpu.make_async_remote_copy(
+        n1 = terms.shape[1] // 2
+        n3 = n1 // (planes * lines)
+        size = planes * n3
+        mine, theirs = core * n1, (1 - core) * n1
+        slots = iter(range(sum_send.shape[1]))
+        pending = []
+
+        def rows_at(at, n):
+            return pl.ds(pl.multiple_of(at, 8), n)
+
+        def remote(src, dst, device):
+            slot = next(slots)
+            copy = pltpu.make_async_remote_copy(
                 src_ref=src, dst_ref=dst, send_sem=sum_send.at[k, slot], recv_sem=sum_recv.at[k, slot],
                 device_id=device, device_id_type=MESH)
-
-        swap = remote(terms.at[k, pl.ds(pl.multiple_of((1 - core) * n1, 8), n1)], r1.at[k], 0, partner)
-        swap.start()
+            copy.start()
+            pending.append(copy)
+            return copy
+
+        far_first = list(range(lines - 1, -1, -1))
+        blocks = [line_peer(d)[1] * size for d in range(lines)]
+        swaps = {
+            d: remote(terms.at[k, rows_at(theirs + blocks[d], size)], r1.at[k, rows_at(blocks[d], size)], partner)
+            for d in far_first
+        }
 
         for c in range(2):
             acc = None
@@ -267,18 +288,37 @@
             grad[k, c] = pick(split(pick(row_place, split(acc))), col_place)
         gpack[k, 0] = paired(upper, grad[k, 0, :, :LANES], grad[k, 1, :, :LANES])
         gpack[k, 1] = paired(lower, grad[k, 0, :, LANES + tile:], grad[k, 1, :, LANES + tile:])
+
+        scatter2 = {}
+        for d in far_first:
+            swaps[d].wait_recv()
+            a1[k, rows_at(blocks[d], size)] = terms[k, rows_at(mine + blocks[d], size)] + r1[k, rows_at(blocks[d], size)]
+            scatter2[d] = []
+            for e in range(1, planes):
+                device, other = plane_peer(e)
+                scatter2[d].append(remote(a1.at[k, rows_at(blocks[d] + other * n3, n3)], r2.at[k, e - 1, d], device))
         start_all(lambda dr, dc: grad_copy(k, dr, dc))
 
-        swap.wait_recv()
-        a1[k] = terms[k, pl.ds(pl.multiple_of(core * n1, 8), n1)] + r1[k]
-        slot = 1
-        scatter2 = []
-        for d in range(1, planes):
-            device, other = plane_peer(d)
-            copy = remote(a1.at[k, pl.ds(pl.multiple_of(other * n2, 8), n2)], r2.at[k, d - 1], slot, device)
-            copy.start()
-            scatter2.append(copy)
-            slot += 1
+        scatter3 = []
+        for d in far_first:
+            value = a1[k, rows_at(blocks[d] + plane * n3, n3)]
+            for e in range(1, planes):
+                scatter2[d][e - 1].wait_recv()
+                value = value + r2[k, e - 1, d]
+            if d:
+                a2[k, d - 1] = value
+                scatter3.append((d, remote(a2.at[k, d - 1], r3.at[k, d - 1], line_peer(d)[0])))
+        for d, copy in scatter3:
+            copy.wait_recv()
+            value = value + r3[k, d - 1]
+        own = rows_at(mine + blocks[0] + plane * n3, n3)
+        weights[k + 1, own] = weights[k, own] - coeff * value
+
+        def chunk(d):
+            return weights.at[k + 1, rows_at(mine + blocks[d] + plane * n3, n3)]
+
+        gather3 = {d: remote(chunk(0), chunk(0), line_peer(d)[0]) for d in far_first[:-1]}
+        gather2 = {0: [remote(chunk(0), chunk(0), plane_peer(e)[0]) for e in range(1, planes)]}
 
         wait_all(lambda dr, dc: grad_copy(k, dr, dc), False)
         target = current if k + 1 < ITERS else new_obj_ref
@@ -300,45 +340,18 @@
             for c in range(2):
                 ext[k + 1, c, H:H + tile, LANES:LANES + tile] = current[c]
 
-        for copy in scatter2:
+        for d in range(1, lines):
+            gather3[d].wait_recv()
+            gather2[d] = [remote(chunk(d), chunk(d), plane_peer(e)[0]) for e in range(1, planes)]
+        back1 = []
+        for d in range(lines):
+            for copy in gather2[d]:
+                copy.wait_recv()
+            block = weights.at[k + 1, rows_at(mine + blocks[d], size)]
+            back1.append(remote(block, block, partner))
+        for copy in back1:
             copy.wait_recv()
-        value = a1[k, pl.ds(pl.multiple_of(plane * n2, 8), n2)]
-        for d in range(1, planes):
-            value = value + r2[k, d - 1]
-        a2[k] = value
-        scatter3 = []
-        for d in range(1, lines):
-            device, other = line_peer(d)
-            copy = remote(a2.at[k, pl.ds(pl.multiple_of(other * n3, 8), n3)], r3.at[k, d - 1], slot, device)
-            copy.start()
-            scatter3.append(copy)
-            slot += 1
-        for copy in scatter3:
-            copy.wait_recv()
-        value = a2[k, pl.ds(pl.multiple_of(line * n3, 8), n3)]
-        for d in range(1, lines):
-            value = value + r3[k, d - 1]
-        at1 = core * n1
-        at2 = at1 + plane * n2
-        at3 = at2 + line * n3
-        mine = pl.ds(pl.multiple_of(at3, 8), n3)
-        weights[k + 1, mine] = weights[k, mine] - coeff * value
-
-        gathers = []
-        for peers, make, at, size in (
-            (lines, line_peer, at3, n3), (planes, plane_peer, at2, n2), (2, lambda d: (partner, None), at1, n1)
-        ):
-            block = weights.at[k + 1, pl.ds(pl.multiple_of(at, 8), size)]
-            stage = []
-            for d in range(1, peers):
-                copy = remote(block, block, slot, make(d)[0])
-                copy.start()
-                stage.append(copy)
-                slot += 1
-            for copy in stage:
-                copy.wait_recv()
-            gathers += stage
-        for copy in [swap] + scatter2 + scatter3 + gathers:
+        for copy in pending:
             copy.wait_send()
         wait_all(lambda dr, dc: halo_copy(k, source, dr, dc), True)
         wait_all(lambda dr, dc: grad_copy(k, dr, dc), True)
@@ -357,9 +370,8 @@
     total = 2 * modes * frame * (frame // LANES)
     planes, lines = rows * 2, cols // 4
     n1 = total // 2
-    n2 = n1 // planes
-    n3 = n2 // lines
-    copies = 2 + 2 * (planes - 1) + 2 * (lines - 1)
+    n3 = n1 // (planes * lines)
+    copies = 2 * (lines * planes + lines - 1)
     f32 = jnp.float32
     wide = 2 * frame
     vmem = pl.BlockSpec(memory_space=pltpu.VMEM)
@@ -391,8 +403,8 @@
             pltpu.VMEM((ITERS, total, LANES), f32),
             pltpu.VMEM((ITERS, n1, LANES), f32),
             pltpu.VMEM((ITERS, n1, LANES), f32),
-            pltpu.VMEM((ITERS, planes - 1, n2, LANES), f32),
-            pltpu.VMEM((ITERS, n2, LANES), f32),
+            pltpu.VMEM((ITERS, planes - 1, lines, n3, LANES), f32),
+            pltpu.VMEM((ITERS, lines - 1, n3, LANES), f32),
             pltpu.VMEM((ITERS, lines - 1, n3, LANES), f32),
             pltpu.VMEM((ITERS + 1, total, LANES), f32),
             dma((ITERS, 8)), dma((ITERS, 8)), dma((ITERS, 8)), dma((ITERS, 8)),

time: 90.2 us -> 77.2 us (0.86)
  Pallas kernels: 86.5 us -> 73.2 us
    pallas_call x1, Pallas kernels: 86.5 us -> 73.2 us  [local(): pl.pallas_call(functools.partial(kernel, rows, cols), out_shape=(jax.Shap...]
where the time goes in v1:
time: 77.2 us; the launch traced here: 76.8 us
  Pallas kernels  73.2 us (95%)
  local copies, waits for them, and re-layouts  2.93 us (4%)
    pallas_call x1, Pallas kernels, local(): pl.pallas_call(functools.partial(kernel, rows, cols), out_shape=(jax.Shap...  73.2 us
    unnamed x4, local copies, waits for them, and re-layouts  2.93 us

profile of v1, /device:TPU:0, one launch (start us, length us, event | category | flops | bytes accessed | tf_op | source)
XLA Modules:
  0.0 76.8 jit_solution(5071999360285700370)
XLA Ops:
  0.6 73.2 %shard_map.68 = (f32[2,256,256]{2,1,0:T(8,128)}, f32[2,2,256,256]{3,2,1,0:T(8,128)}) custom-call(f32[2,256,256]{2,1,0:T(8,128)} %obj_ref.1, f32[2,2,256,256]{3,2,1,0:T(8,128)} %probe_ref.1, f32[1,1,1,256,256]{4,3,2,1,0:T(8,128)} %amp_ref.1, bf16[4,256,256]{2,1,0:T(8,128)(2,1)} %constant.2.clone.tables_ref, s32[1,1,1,2]{3,2,1,0:T(1,128)} %off_ref.1), custom_call_target="tpu_custom_call" | custom-call | tf_op jit(solution)/shard_map/pallas_call | solution.py:379
  73.9 0.0 copy-start
  73.9 2.0 %copy.9 = f32[2,256,256]{2,1,0:T(8,128)} copy(f32[2,256,256]{2,1,0:T(8,128)} %get-tuple-element.4) | data formatting | bytes 1048576
  75.8 0.0 copy-done
  75.8 1.0 %copy.10 = f32[2,2,256,256]{3,2,1,0:T(8,128)} copy(f32[2,2,256,256]{3,2,1,0:T(8,128)S(1)} %copy-done) | data formatting | bytes 2097152
Async XLA Ops:
  73.9 2.0 %copy-start = (f32[2,2,256,256]{3,2,1,0:T(8,128)S(1)}, f32[2,2,256,256]{3,2,1,0:T(8,128)}, u32[]{:S(2)}) copy-start(f32[2,2,256,256]{3,2,1,0:T(8,128)} %get-tuple-element.5) | copy-start | bytes 3145732

commit v2 on v1

--- a/solution.py
+++ b/solution.py
@@ -49,16 +49,18 @@
 
 
 def kernel(
-    rows, cols, obj_ref, probe_ref, amp_ref, tables_ref, off_ref,
+    rows, cols, obj_in, probe_in, amp_in, tables_in, off_ref,
     new_obj_ref, new_probe_ref,
     a_hi, a_lo, b_hi, b_lo, x_hi, x_lo,
     row_pick, col_pick, row_place, col_place, ext, side, pack, grad, gpack, grows, gside, gcorner, current,
     terms, r1, a1, r2, a2, r3, weights,
+    amp_ref, tables_ref, in_sem, out_sem,
     halo_send, halo_recv, grad_send, grad_recv, sum_send, sum_recv,
 ):
-    frame = amp_ref.shape[-1]
-    tile = obj_ref.shape[1]
-    modes = probe_ref.shape[1]
+    frame = amp_in.shape[-1]
+    tile = obj_in.shape[1]
+    modes = probe_in.shape[1]
+    half = frame // LANES
     span = tile + 2 * H
     row, col = lax.axis_index("row"), lax.axis_index("col")
     coeff = probe_step / (rows * cols)
@@ -96,11 +98,26 @@
 
     partner = (row, col + 1 - 2 * core)
 
-    ext[...] = jnp.zeros_like(ext)
-    side[...] = jnp.zeros_like(side)
-    grows[...] = jnp.zeros_like(grows)
-    gside[...] = jnp.zeros_like(gside)
-    gcorner[...] = jnp.zeros_like(gcorner)
+    def strip(ref, c, m, h):
+        return ref.at[c, m, :, pl.ds(h * LANES, LANES)]
+
+    def strip_rows(c, m, h):
+        return pl.ds(((c * modes + m) * half + h) * frame, frame)
+
+    strips = [(m, h) for m in range(modes) for h in range(half)]
+    load_obj = pltpu.make_async_copy(obj_in, current.at[0], in_sem.at[0])
+    loads = [
+        pltpu.make_async_copy(tables_in, tables_ref, in_sem.at[1]),
+        pltpu.make_async_copy(amp_in.at[0, 0, 0], amp_ref, in_sem.at[2]),
+    ]
+    for c in range(2):
+        for n, (m, h) in enumerate(strips):
+            loads.append(pltpu.make_async_copy(
+                strip(probe_in, c, m, h), weights.at[0, strip_rows(c, m, h)],
+                in_sem.at[3 + c * len(strips) + n]))
+    load_obj.start()
+    for copy in loads:
+        copy.start()
 
     barrier = pltpu.get_barrier_semaphore()
     for dr, dc in around:
@@ -123,8 +140,7 @@
         pack[k, 0] = paired(lower, src[0, :, :LANES], src[1, :, :LANES])
         pack[k, 1] = paired(upper, src[0, :, tile - LANES:], src[1, :, tile - LANES:])
 
-    def halo_copy(k, src, dr, dc):
-        n = around.index((dr, dc))
+    def halo_ends(k, src, dr, dc):
         if dc == 0:
             source = src.at[:, pl.ds(0 if dr < 0 else tile - H, H), :]
             target = ext.at[k, :, pl.ds(tile + H if dr < 0 else 0, H), pl.ds(LANES, tile)]
@@ -133,12 +149,16 @@
             at, size = {-1: (0, H), 0: (0, tile), 1: (tile - H, H)}[dr]
             source = pack.at[k, which, pl.ds(at, size)]
             target = side.at[k, 1 - which, pl.ds({-1: tile + H, 0: H, 1: 0}[dr], size)]
+        return source, target
+
+    def halo_copy(k, src, dr, dc):
+        n = around.index((dr, dc))
+        source, target = halo_ends(k, src, dr, dc)
         return pltpu.make_async_remote_copy(
             src_ref=source, dst_ref=target, send_sem=halo_send.at[k, n], recv_sem=halo_recv.at[k, n],
             device_id=(row + dr, col + dc), device_id_type=MESH)
 
-    def grad_copy(k, dr, dc):
-        n = around.index((dr, dc))
+    def grad_ends(k, dr, dc):
         if dc == 0:
             source = grad.at[k, :, pl.ds(0 if dr < 0 else tile + H, H), pl.ds(LANES, tile)]
             target = grows.at[k, 0 if dr > 0 else 1]
@@ -150,6 +170,11 @@
                 target = gside.at[k, 1 - which]
             else:
                 target = gcorner.at[k, 1 - which, 0 if dr > 0 else 1]
+        return source, target
+
+    def grad_copy(k, dr, dc):
+        n = around.index((dr, dc))
+        source, target = grad_ends(k, dr, dc)
         return pltpu.make_async_remote_copy(
             src_ref=source, dst_ref=target, send_sem=grad_send.at[k, n], recv_sem=grad_recv.at[k, n],
             device_id=(row + dr, col + dc), device_id_type=MESH)
@@ -171,12 +196,25 @@
                 def _(dr=dr, dc=dc):
                     make(dr, dc).wait_recv()
 
-    pack_tile(0, obj_ref)
+    load_obj.wait()
+    pack_tile(0, current.at[0])
     tall = 1 + (row > 0).astype(jnp.int32) + (row < rows - 1).astype(jnp.int32)
     broad = 1 + (col > 0).astype(jnp.int32) + (col < cols - 1).astype(jnp.int32)
     pl.semaphore_wait(barrier, tall * broad - 1 + planes + lines - 1)
-    start_all(lambda dr, dc: halo_copy(0, obj_ref, dr, dc))
-
+    start_all(lambda dr, dc: halo_copy(0, current.at[0], dr, dc))
+
+    def zero(ref):
+        ref[...] = jnp.zeros_like(ref)
+
+    for dr, dc in around:
+        @pl.when(jnp.logical_not(inside(-dr, -dc)))
+        def _(dr=dr, dc=dc):
+            for k in range(ITERS):
+                zero(halo_ends(k, current.at[0], dr, dc)[1])
+                zero(grad_ends(k, dr, dc)[1])
+
+    for copy in loads:
+        copy.wait()
     for n, (a, b) in enumerate(((a_hi, b_hi), (a_lo, b_lo))):
         real, imag = tables_ref[n], tables_ref[2 + n]
         lo, hi = pl.ds(0, frame), pl.ds(frame, frame)
@@ -185,13 +223,8 @@
             ref[hi, hi] = real
             ref[lo, hi] = -imag if sign > 0 else imag
             ref[hi, lo] = imag if sign > 0 else -imag
-    half = frame // LANES
     for c in range(2):
-        ext[0, c, H:H + tile, LANES:LANES + tile] = obj_ref[c]
-        for m in range(modes):
-            for h in range(half):
-                weights[0, pl.ds(((c * modes + m) * half + h) * frame, frame)] = (
-                    probe_ref[c, m, :, h * LANES:(h + 1) * LANES])
+        ext[0, c, H:H + tile, LANES:LANES + tile] = current[0, c]
 
     def probe_part(k, c, m):
         base = (c * modes + m) * half
@@ -207,7 +240,7 @@
         ref[...] = jnp.where(outer_at == inner_at + shift, 1.0, 0.0).astype(bf16)
 
     for k in range(ITERS):
-        source = obj_ref if k == 0 else current
+        source = current.at[k]
         wait_all(lambda dr, dc: halo_copy(k, source, dr, dc), False)
         for s, at in ((0, 0), (1, LANES + tile)):
             block = side[k, s]
@@ -235,7 +268,7 @@
         far = product((x_hi, x_lo), (b_hi, b_lo))
         far = [[far[m * frame:(m + 1) * frame, c * frame:(c + 1) * frame] for c in range(2)] for m in range(modes)]
         intensity = sum(re * re + im * im for re, im in far)
-        factor = 1.0 - amp_ref[0, 0, 0] / jnp.sqrt(intensity + 1.0)
+        factor = 1.0 - amp_ref[...] / jnp.sqrt(intensity + 1.0)
         for m in range(modes):
             for c in range(2):
                 x_hi[cut(m), cut(c)], x_lo[cut(m), cut(c)] = split(far[m][c] * factor)
@@ -321,7 +354,7 @@
         gather2 = {0: [remote(chunk(0), chunk(0), plane_peer(e)[0]) for e in range(1, planes)]}
 
         wait_all(lambda dr, dc: grad_copy(k, dr, dc), False)
-        target = current if k + 1 < ITERS else new_obj_ref
+        target = current.at[k + 1]
         for s in range(2):
             mask, at = ((lower, 0), (upper, tile - LANES))[s]
             block = gside[k, s]
@@ -335,11 +368,13 @@
         for c in range(2):
             target[c] = source[c] - object_step * grad[k, c, H:H + tile, LANES:LANES + tile]
         if k + 1 < ITERS:
-            pack_tile(k + 1, current)
-            start_all(lambda dr, dc: halo_copy(k + 1, current, dr, dc))
+            pack_tile(k + 1, target)
+            start_all(lambda dr, dc: halo_copy(k + 1, target, dr, dc))
             for c in range(2):
-                ext[k + 1, c, H:H + tile, LANES:LANES + tile] = current[c]
-
+                ext[k + 1, c, H:H + tile, LANES:LANES + tile] = target[c]
+        else:
+            store_obj = pltpu.make_async_copy(target, new_obj_ref, out_sem.at[0])
+            store_obj.start()
         for d in range(1, lines):
             gather3[d].wait_recv()
             gather2[d] = [remote(chunk(d), chunk(d), plane_peer(e)[0]) for e in range(1, planes)]
@@ -349,6 +384,14 @@
                 copy.wait_recv()
             block = weights.at[k + 1, rows_at(mine + blocks[d], size)]
             back1.append(remote(block, block, partner))
+        if k + 1 == ITERS:
+            stores = [
+                pltpu.make_async_copy(
+                    weights.at[ITERS, strip_rows(core, m, h)], strip(new_probe_ref, core, m, h), out_sem.at[1 + n])
+                for n, (m, h) in enumerate(strips)
+            ]
+            for copy in stores:
+                copy.start()
         for copy in back1:
             copy.wait_recv()
         for copy in pending:
@@ -356,9 +399,15 @@
         wait_all(lambda dr, dc: halo_copy(k, source, dr, dc), True)
         wait_all(lambda dr, dc: grad_copy(k, dr, dc), True)
 
-    for c in range(2):
-        for m in range(modes):
-            new_probe_ref[c, m] = probe_part(ITERS, c, m)
+    for n, (m, h) in enumerate(strips):
+        copy = pltpu.make_async_copy(
+            weights.at[ITERS, strip_rows(1 - core, m, h)], strip(new_probe_ref, 1 - core, m, h),
+            out_sem.at[1 + len(strips) + n])
+        copy.start()
+        stores.append(copy)
+    store_obj.wait()
+    for copy in stores:
+        copy.wait()
 
 
 def local(rows, cols, object_field, probe, amplitudes, offsets):
@@ -374,7 +423,8 @@
     copies = 2 * (lines * planes + lines - 1)
     f32 = jnp.float32
     wide = 2 * frame
-    vmem = pl.BlockSpec(memory_space=pltpu.VMEM)
+    anywhere = pl.BlockSpec(memory_space=pl.ANY)
+    strips = modes * (frame // LANES)
     dma = pltpu.SemaphoreType.DMA
     return pl.pallas_call(
         functools.partial(kernel, rows, cols),
@@ -382,8 +432,8 @@
             jax.ShapeDtypeStruct(object_field.shape, f32),
             jax.ShapeDtypeStruct(probe.shape, f32),
         ),
-        in_specs=[vmem] * 4 + [pl.BlockSpec(memory_space=pltpu.SMEM)],
-        out_specs=(vmem, vmem),
+        in_specs=[anywhere] * 4 + [pl.BlockSpec(memory_space=pltpu.SMEM)],
+        out_specs=(anywhere, anywhere),
         scratch_shapes=[
             *[pltpu.VMEM((wide, wide), bf16)] * 4,
             *[pltpu.VMEM((wide, modes * frame), bf16)] * 2,
@@ -399,7 +449,7 @@
             pltpu.VMEM((ITERS, 2, 2, H, tile), f32),
             pltpu.VMEM((ITERS, 2, tile, LANES), f32),
             pltpu.VMEM((ITERS, 2, 2, H, LANES), f32),
-            pltpu.VMEM((2, tile, tile), f32),
+            pltpu.VMEM((ITERS + 1, 2, tile, tile), f32),
             pltpu.VMEM((ITERS, total, LANES), f32),
             pltpu.VMEM((ITERS, n1, LANES), f32),
             pltpu.VMEM((ITERS, n1, LANES), f32),
@@ -407,6 +457,9 @@
             pltpu.VMEM((ITERS, lines - 1, n3, LANES), f32),
             pltpu.VMEM((ITERS, lines - 1, n3, LANES), f32),
             pltpu.VMEM((ITERS + 1, total, LANES), f32),
+            pltpu.VMEM((frame, frame), f32),
+            pltpu.VMEM((4, frame, frame), bf16),
+            dma((3 + 2 * strips,)), dma((1 + 2 * strips,)),
             dma((ITERS, 8)), dma((ITERS, 8)), dma((ITERS, 8)), dma((ITERS, 8)),
             dma((ITERS, copies)), dma((ITERS, copies)),
         ],

time: 77.2 us -> 75.8 us (0.982)
  Pallas kernels: 73.2 us -> 72 us
    pallas_call x1, Pallas kernels: 73.2 us -> 72 us  [local(): pl.pallas_call(functools.partial(kernel, rows, cols), out_shape=(jax.Shap...]
where the time goes in v2:
time: 75.8 us; the launch traced here: 75.6 us
  Pallas kernels  72 us (95%)
  local copies, waits for them, and re-layouts  2.93 us (4%)
    pallas_call x1, Pallas kernels, local(): pl.pallas_call(functools.partial(kernel, rows, cols), out_shape=(jax.Shap...  72 us
    unnamed x4, local copies, waits for them, and re-layouts  2.93 us

profile of v2, /device:TPU:0, one launch (start us, length us, event | category | flops | bytes accessed | tf_op | source)
XLA Modules:
  0.0 75.6 jit_solution(1631793679143646608)
XLA Ops:
  0.6 72.0 %shard_map.68 = (f32[2,256,256]{2,1,0:T(8,128)}, f32[2,2,256,256]{3,2,1,0:T(8,128)}) custom-call(f32[2,256,256]{2,1,0:T(8,128)} %obj_in.1, f32[2,2,256,256]{3,2,1,0:T(8,128)} %probe_in.1, f32[1,1,1,256,256]{4,3,2,1,0:T(8,128)} %amp_in.1, bf16[4,256,256]{2,1,0:T(8,128)(2,1)} %constant.2.clone.tables_in, s32[1,1,1,2]{3,2,1,0:T(1,128)} %off_ref.1), custom_call_target="tpu_custom_call" | custom-call | tf_op jit(solution)/shard_map/pallas_call | solution.py:429
  72.7 0.0 copy-start
  72.7 2.0 %copy.9 = f32[2,256,256]{2,1,0:T(8,128)} copy(f32[2,256,256]{2,1,0:T(8,128)} %get-tuple-element.4) | data formatting | bytes 1048576
  74.7 0.0 copy-done
  74.7 1.0 %copy.10 = f32[2,2,256,256]{3,2,1,0:T(8,128)} copy(f32[2,2,256,256]{3,2,1,0:T(8,128)S(1)} %copy-done) | data formatting | bytes 2097152
Async XLA Ops:
  72.7 2.0 %copy-start = (f32[2,2,256,256]{3,2,1,0:T(8,128)S(1)}, f32[2,2,256,256]{3,2,1,0:T(8,128)}, u32[]{:S(2)}) copy-start(f32[2,2,256,256]{3,2,1,0:T(8,128)} %get-tuple-element.5) | copy-start | bytes 3145732
